TPU v7x, 32 devices: a whole 2x2x4 slice. The times are simulated.
32 devices in a mesh: scene: 4 (over y, x), row: 4 (over z), col: 2 (over core).
Axes of the slice: x: 2, y: 2, z: 4, core: 2. Of those that a mesh axis runs over, the one named last changes fastest.
Arguments:
- scenes: bfloat16 [4, 256, 128, 128], P('scene', 'row', 'col'), may hold values from -6 to 6
- cotangent: bfloat16 [4, 256, 128, 128], P('scene', 'row', 'col'), may hold values from -0.016479492 to 0.016479492
- params: float32 [294912], P(('scene', 'row', 'col')), may hold values from -0.1875 to 0.1875
- partials: float32 [32, 294912], P(('scene', 'row', 'col')), may hold values from -8 to 8
Outputs:
- sam_grad: float32 [294912], P(('scene', 'row', 'col'))
All inputs are finite; a program needn't handle non-finite values.
Results may differ from a plain program's by a relative error of at most 0.0042.
Values may be sent and summed in bfloat16 or wider, within the bound.
A program may use at most 64 MiB of HBM per device.

v0:
```python
import jax
import jax.numpy as jnp
from jax import lax
from jax.sharding import PartitionSpec as P

radius = 2.0
epsilon = 1e-06


def with_halo(cells, sides, width):
    for axis, dim in sides:
        count = lax.axis_size(axis)
        ends = count - 1
        head = lax.slice_in_dim(cells, 0, width, axis=dim)
        tail = lax.slice_in_dim(cells, cells.shape[dim] - width, cells.shape[dim], axis=dim)
        cells = jnp.concatenate(
            [
                lax.ppermute(tail, axis, [(i, (i + 1) % count) for i in range(ends)]),
                cells,
                lax.ppermute(head, axis, [((i + 1) % count, i) for i in range(ends)]),
            ],
            axis=dim,
        )
    return cells


def convolve(padded, kernel):
    return lax.conv_general_dilated(
        padded,
        kernel,
        (1, 1),
        "VALID",
        dimension_numbers=("NHWC", "HWIO", "NHWC"),
        preferred_element_type=jnp.float32,
    )


def widened(field):
    return with_halo(field, (("row", 1), ("col", 2)), 1)


def kernel_grad(padded, errors):
    height = errors.shape[1]
    width = errors.shape[2]
    rows_out = []
    for row_off in range(3):
        cols_out = []
        for col_off in range(3):
            window = padded[:, row_off : row_off + height, col_off : col_off + width, :]
            cols_out.append(
                jnp.einsum("nhwc,nhwd->cd", window, errors, preferred_element_type=jnp.float32)
            )
        rows_out.append(jnp.stack(cols_out))
    return jnp.stack(rows_out)


def on_device(scenes, cotangent, params, partials):
    local_part = partials[0]
    totals = lax.psum(local_part, ("scene", "row", "col"))
    raw_whole = lax.all_gather(params, ("scene", "row", "col"), axis=0, tiled=True)
    factor = radius / (jnp.sqrt(jnp.sum(totals * totals)) + epsilon)
    whole = (raw_whole + factor * totals).astype(jnp.bfloat16)
    channels = scenes.shape[3]
    kernels = whole.reshape(2, 3, 3, channels, channels)
    kernel_one = kernels[0]
    flipped = jnp.transpose(kernels[1][::-1, ::-1], (0, 1, 3, 2))
    padded_in = widened(scenes)
    pre = convolve(padded_in, kernel_one)
    hidden = jax.nn.silu(pre).astype(jnp.bfloat16)
    back = convolve(widened(cotangent), flipped)
    squash = jax.nn.sigmoid(pre)
    delta = (back * squash * (1.0 + pre * (1.0 - squash))).astype(jnp.bfloat16)
    grad_one = kernel_grad(padded_in, delta)
    grad_two = kernel_grad(widened(hidden), cotangent)
    local_grad = jnp.stack([grad_one, grad_two]).reshape(-1)
    return lax.psum_scatter(local_grad, ("scene", "row", "col"), scatter_dimension=0, tiled=True)


def solution(mesh):
    return jax.shard_map(
        on_device,
        mesh=mesh,
        in_specs=(
            P("scene", "row", "col", None),
            P("scene", "row", "col", None),
            P(("scene", "row", "col")),
            P(("scene", "row", "col"), None),
        ),
        out_specs=P(("scene", "row", "col")),
        check_vma=False,
    )
```

profile of v0, /device:TPU:0, one launch (start us, length us, event | category | flops | bytes accessed | tf_op | source)
XLA Modules:
  0.0 384.6 jit_solution(3427847306633833855)
XLA Ops:
  8.1 5.1 %collective-permute-start = (bf16[1,1,64,128]{3,2,1,0:T(8,128)(2,1)S(1)}, bf16[1,1,64,128]{3,2,1,0:T(8,128)(2,1)S(1)}, u32[]{:S(2)}, u32[]{:S(2)}) collective-permute-start(bf16[1,1,64,128]{3,2,1,0:T(8,128)(2,1)S(1)} %get-tuple-element.18), channel_id=1, source_target_pairs={{0,2},{2,4},{4,6},{1,3},{3,5},{5,7},{8,10},{10,12},{12,14},{9,11},... | collective-permute-start | bytes 49160 | tf_op jit(solution)/shard_map/ppermute | solution.py:18
  15.2 4.5 %collective-permute-start.3 = (bf16[1,1,64,128]{3,2,1,0:T(8,128)(2,1)S(1)}, bf16[1,1,64,128]{3,2,1,0:T(8,128)(2,1)S(1)}, u32[]{:S(2)}, u32[]{:S(2)}) collective-permute-start(bf16[1,1,64,128]{3,2,1,0:T(8,128)(2,1)S(1)} %get-tuple-element.16), channel_id=1, source_target_pairs={{0,2},{2,4},{4,6},{1,3},{3,5},{5,7},{8,10},{10,12},{12,14},{9,11},... | collective-permute-start | bytes 49160 | tf_op jit(solution)/shard_map/ppermute | solution.py:18
  25.5 2.9 collective-permute-start.5
  34.5 112.6 %all-reduce.4.cloned.1.call-done = f32[294912]{0:T(1024)} async-done(((f32[294912]{0:T(1024)}), f32[294912]{0:T(1024)}) %all-reduce.4.cloned.1.call-update) | async-done | bytes 1179664 | tf_op jit(solution)/shard_map/psum | solution.py:59
  147.1 2.3 multiply_reduce_fusion
  150.2 53.1 %all-gather.2.cloned.1.call-done = f32[294912]{0:T(1024)} async-done(((f32[9216]{0:T(1024)}), f32[294912]{0:T(1024)}) %all-gather.2.cloned.1.call-update) | async-done | bytes 1179664 | tf_op jit(solution)/shard_map/all_gather | solution.py:60
  203.2 1.5 add_convert_fusion
  204.8 3.2 multiply_convert_fusion.1
  209.4 3.4 multiply_convert_fusion
  214.4 1.3 convolution_bitcast_fusion.13
  215.8 2.5 collective-permute-start.8
  218.4 1.6 collective-permute-start.9
  220.0 2.1 convolution_bitcast_fusion.4
  222.1 1.4 convolution_bitcast_fusion.11
  223.5 1.4 convolution_bitcast_fusion.9
  224.9 1.3 convolution_bitcast_fusion.10
  226.2 1.4 convolution_bitcast_fusion.14
  227.6 1.4 convolution_bitcast_fusion.12
  229.0 1.4 convolution_bitcast_fusion.17
  230.4 1.4 convolution_bitcast_fusion.15
  231.8 1.3 convolution_bitcast_fusion.16
  234.3 1.8 collective-permute-start.10
  244.2 132.5 %all-reduce.6.cloned.1.call-done = f32[294912]{0:T(1024)} async-done(((f32[294912]{0:T(1024)}), f32[294912]{0:T(1024)}) %all-reduce.6.cloned.1.call-update) | async-done | bytes 1179664
  376.7 1.4 dynamic-slice
  (106 shorter events, 27.2 us)
Async XLA Ops:
  6.5 1.5 copy-start.3
  6.5 140.6 %all-reduce.4.cloned.1.call-start = ((), (), s32[]{:S(2)}) async-start(), calls=%async_computation.1 | async-start | bytes 2359296 | tf_op jit(solution)/shard_map/psum | solution.py:59
  7.3 196.0 %all-gather.2.cloned.1.call-start = ((), (), s32[]{:S(2)}) async-start(), calls=%async_computation | async-start | bytes 1216512 | tf_op jit(solution)/shard_map/all_gather | solution.py:60
  8.0 368.7 %all-reduce.6.cloned.1.call-start = ((), (), s32[]{:S(2)}) async-start(), calls=%async_computation.2 | async-start | bytes 2359296
  8.1 17.1 %copy-start.5 = (bf16[1,64,64,128]{3,2,1,0:T(8,128)(2,1)S(1)}, bf16[1,64,64,128]{3,2,1,0:T(8,128)(2,1)}, u32[]{:S(2)}) copy-start(bf16[1,64,64,128]{3,2,1,0:T(8,128)(2,1)} %param.5) | copy-start | bytes 3145732
  8.1 13.0 %collective-permute-start = (bf16[1,1,64,128]{3,2,1,0:T(8,128)(2,1)S(1)}, bf16[1,1,64,128]{3,2,1,0:T(8,128)(2,1)S(1)}, u32[]{:S(2)}, u32[]{:S(2)}) collective-permute-start(bf16[1,1,64,128]{3,2,1,0:T(8,128)(2,1)S(1)} %get-tuple-element.18), channel_id=1, source_target_pairs={{0,2},{2,4},{4,6},{1,3},{3,5},{5,7},{8,10},{10,12},{12,14},{9,11},... | collective-permute-start | bytes 49160 | tf_op jit(solution)/shard_map/ppermute | solution.py:18
  13.2 8.6 %collective-permute-start.1 = (bf16[1,1,64,128]{3,2,1,0:T(8,128)(2,1)S(1)}, bf16[1,1,64,128]{3,2,1,0:T(8,128)(2,1)S(1)}, u32[]{:S(2)}, u32[]{:S(2)}) collective-permute-start(bf16[1,1,64,128]{3,2,1,0:T(8,128)(2,1)S(1)} %get-tuple-element.17), channel_id=1, source_target_pairs={{2,0},{4,2},{6,4},{3,1},{5,3},{7,5},{10,8},{12,10},{14,12},{11,9},... | collective-permute-start | bytes 49160 | tf_op jit(solution)/shard_map/ppermute | solution.py:20
  15.2 9.9 %collective-permute-start.3 = (bf16[1,1,64,128]{3,2,1,0:T(8,128)(2,1)S(1)}, bf16[1,1,64,128]{3,2,1,0:T(8,128)(2,1)S(1)}, u32[]{:S(2)}, u32[]{:S(2)}) collective-permute-start(bf16[1,1,64,128]{3,2,1,0:T(8,128)(2,1)S(1)} %get-tuple-element.16), channel_id=1, source_target_pairs={{0,2},{2,4},{4,6},{1,3},{3,5},{5,7},{8,10},{10,12},{12,14},{9,11},... | collective-permute-start | bytes 49160 | tf_op jit(solution)/shard_map/ppermute | solution.py:18
  19.8 5.6 %collective-permute-start.4 = (bf16[1,1,64,128]{3,2,1,0:T(8,128)(2,1)S(1)}, bf16[1,1,64,128]{3,2,1,0:T(8,128)(2,1)S(1)}, u32[]{:S(2)}, u32[]{:S(2)}) collective-permute-start(bf16[1,1,64,128]{3,2,1,0:T(8,128)(2,1)S(1)} %get-tuple-element.15), channel_id=1, source_target_pairs={{2,0},{4,2},{6,4},{3,1},{5,3},{7,5},{10,8},{12,10},{14,12},{11,9},... | collective-permute-start | bytes 49160 | tf_op jit(solution)/shard_map/ppermute | solution.py:20
  22.5 7.2 %collective-permute-start.2 = (bf16[1,66,1,128]{3,2,1,0:T(2,128)(2,1)S(1)}, bf16[1,66,1,128]{3,2,1,0:T(2,128)(2,1)S(1)}, u32[]{:S(2)}, u32[]{:S(2)}) collective-permute-start(bf16[1,66,1,128]{3,2,1,0:T(2,128)(2,1)S(1)} %get-tuple-element.13), channel_id=1, source_target_pairs={{0,1},{2,3},{4,5},{6,7},{8,9},{10,11},{12,13},{14,15},{16,17},{18,... | collective-permute-start | bytes 50696 | tf_op jit(solution)/shard_map/ppermute | solution.py:18
  23.8 5.9 %collective-permute-start.7 = (bf16[1,66,1,128]{3,2,1,0:T(2,128)(2,1)S(1)}, bf16[1,66,1,128]{3,2,1,0:T(2,128)(2,1)S(1)}, u32[]{:S(2)}, u32[]{:S(2)}) collective-permute-start(bf16[1,66,1,128]{3,2,1,0:T(2,128)(2,1)S(1)} %get-tuple-element.14), channel_id=1, source_target_pairs={{1,0},{3,2},{5,4},{7,6},{9,8},{11,10},{13,12},{15,14},{17,16},{19,... | collective-permute-start | bytes 50696 | tf_op jit(solution)/shard_map/ppermute | solution.py:20
  25.5 6.1 %collective-permute-start.5 = (bf16[1,66,1,128]{3,2,1,0:T(2,128)(2,1)S(1)}, bf16[1,66,1,128]{3,2,1,0:T(2,128)(2,1)S(1)}, u32[]{:S(2)}, u32[]{:S(2)}) collective-permute-start(bf16[1,66,1,128]{3,2,1,0:T(2,128)(2,1)S(1)} %get-tuple-element.7), channel_id=1, source_target_pairs={{0,1},{2,3},{4,5},{6,7},{8,9},{10,11},{12,13},{14,15},{16,17},{18,... | collective-permute-start | bytes 50696 | tf_op jit(solution)/shard_map/ppermute | solution.py:18
  28.4 3.2 collective-permute-start.6
  147.1 56.1 %copy-start = (f32[294912]{0:T(1024)S(1)}, f32[294912]{0:T(1024)}, u32[]{:S(2)}) copy-start(f32[294912]{0:T(1024)} %all-reduce.4.cloned.1.call-done) | copy-start | bytes 3538948
  150.1 54.7 %copy-start.15 = (pred[8,9]{0,1:T(8,128)(4,1)S(1)}, pred[8,9]{0,1:T(8,128)(4,1)}, u32[]{:S(2)}) copy-start(pred[8,9]{0,1:T(8,128)(4,1)} %constant.21) | copy-start | bytes 220
  203.2 1.6 copy-start.9
  215.8 18.3 %collective-permute-start.8 = (bf16[1,1,64,128]{3,2,1,0:T(8,128)(2,1)S(1)}, bf16[1,1,64,128]{3,2,1,0:T(8,128)(2,1)S(1)}, u32[]{:S(2)}, u32[]{:S(2)}) collective-permute-start(bf16[1,1,64,128]{3,2,1,0:T(8,128)(2,1)S(1)} %slice.186), channel_id=1, source_target_pairs={{0,2},{2,4},{4,6},{1,3},{3,5},{5,7},{8,10},{10,12},{12,14},{9,11},... | collective-permute-start | bytes 49160 | tf_op jit(solution)/shard_map/ppermute | solution.py:18
  218.3 3.7 copy-start.8
  218.4 15.8 %collective-permute-start.9 = (bf16[1,1,64,128]{3,2,1,0:T(8,128)(2,1)S(1)}, bf16[1,1,64,128]{3,2,1,0:T(8,128)(2,1)S(1)}, u32[]{:S(2)}, u32[]{:S(2)}) collective-permute-start(bf16[1,1,64,128]{3,2,1,0:T(8,128)(2,1)S(1)} %slice.189), channel_id=1, source_target_pairs={{2,0},{4,2},{6,4},{3,1},{5,3},{7,5},{10,8},{12,10},{14,12},{11,9},... | collective-permute-start | bytes 49160 | tf_op jit(solution)/shard_map/ppermute | solution.py:20
  223.5 1.4 copy-start.14
  230.4 1.4 copy-start.12
  233.2 4.2 %copy-start.6 = (bf16[1,64,64,128]{3,2,1,0:T(8,128)(2,1)S(1)}, bf16[1,64,64,128]{3,2,1,0:T(8,128)(2,1)}, u32[]{:S(2)}) copy-start(bf16[1,64,64,128]{3,2,1,0:T(8,128)(2,1)} %param.5) | copy-start | bytes 3145732
  234.3 4.1 %collective-permute-start.10 = (bf16[1,66,1,128]{3,2,1,0:T(2,128)(2,1)S(1)}, bf16[1,66,1,128]{3,2,1,0:T(2,128)(2,1)S(1)}, u32[]{:S(2)}, u32[]{:S(2)}) collective-permute-start(bf16[1,66,1,128]{3,2,1,0:T(2,128)(2,1)S(1)} %get-tuple-element.11), channel_id=1, source_target_pairs={{0,1},{2,3},{4,5},{6,7},{8,9},{10,11},{12,13},{14,15},{16,17},{18,... | collective-permute-start | bytes 50696 | tf_op jit(solution)/shard_map/ppermute | solution.py:18
  236.1 3.1 collective-permute-start.11
  (7 other events, 7.4 us)
Sparse Core Ops, SparseCore 0:
  12.7 134.3 all-reduce.3
  150.1 53.0 all-gather.1
  244.3 132.3 all-reduce.5
where the time goes:
time: 385 us
  waiting for transfers between devices  301 us (78%)
  starting transfers between devices  26.3 us (7%)
  matrix products  24.9 us (6%)
  between operations  14.5 us (4%)
  local copies, waits for them, and re-layouts  11.1 us (3%)
  other arithmetic  7.21 us (2%)
    unnamed x4, waiting for transfers between devices  134 us
    psum x1, waiting for transfers between devices, on_device(): totals = lax.psum(local_part, ('scene', 'row', 'col'))  113 us
    all_gather x1, waiting for transfers between devices, on_device(): lax.all_gather(params, ('scene', 'row', 'col'), axis=0, tiled=True)  53.1 us
    dot_general x18, matrix products, kernel_grad(): jnp.einsum('nhwc,nhwd->cd', window, errors, preferred_element_type=jnp.fl...  18.2 us
    ppermute x6, starting transfers between devices, with_halo(): lax.ppermute(tail, axis, [(i, (i + 1) % count) for i in range(ends)])  18.1 us
    ppermute x6, starting transfers between devices, with_halo(): lax.ppermute(head, axis, [((i + 1) % count, i) for i in range(ends)])  8.06 us
  transfers between devices with their start and end apart: 15, of which 5 were waited for; matrix products, arithmetic and copies ran while one was open for 6% of the time, Pallas kernels for 0%

commit v1 on v0

--- a/solution.py
+++ b/solution.py
@@ -57,7 +57,15 @@
 def on_device(scenes, cotangent, params, partials):
     local_part = partials[0]
     totals = lax.psum(local_part, ("scene", "row", "col"))
-    raw_whole = lax.all_gather(params, ("scene", "row", "col"), axis=0, tiled=True)
+    ways, here = (lax.axis_size(("scene", "row", "col")), lax.axis_index(("scene", "row", "col")))
+    grown, reach = (params, 1)
+    while reach < ways:
+        theirs = lax.ppermute(grown, ("scene", "row", "col"), [(d, d ^ reach) for d in range(ways)])
+        mine_first = jnp.concatenate([grown, theirs], axis=0)
+        theirs_first = jnp.concatenate([theirs, grown], axis=0)
+        grown = jnp.where(here & reach == 0, mine_first, theirs_first)
+        reach = 2 * reach
+    raw_whole = grown
     factor = radius / (jnp.sqrt(jnp.sum(totals * totals)) + epsilon)
     whole = (raw_whole + factor * totals).astype(jnp.bfloat16)
     channels = scenes.shape[3]

time: 385 us -> 334 us (0.87)
  waiting for transfers between devices: 301 us -> 241 us
  starting transfers between devices: 26.3 us -> 35.8 us
    all_gather x1 -> x0, waiting for transfers between devices: 53.1 us -> none  [on_device(): lax.all_gather(params, ('scene', 'row', 'col'), axis=0, tiled=True)]
    psum x1, waiting for transfers between devices: 113 us -> 96.1 us  [on_device(): totals = lax.psum(local_part, ('scene', 'row', 'col'))]
    ppermute x0 -> x5, waiting for transfers between devices: none -> 11.7 us  [on_device(): lax.ppermute(grown, ('scene', 'row', 'col'), [(d, d ^ reach) for d in ran...]
    ppermute x0 -> x5, starting transfers between devices: none -> 9.15 us  [on_device(): lax.ppermute(grown, ('scene', 'row', 'col'), [(d, d ^ reach) for d in ran...]
    unnamed x4 -> x3, waiting for transfers between devices: 134 us -> 132 us
  transfers between devices with their start and end apart: 15 -> 19, of which waited for: 5 -> 6; matrix products, arithmetic and copies ran while one was open for 6% -> 6% of each run, Pallas kernels for 0% -> 0%
where the time goes in v1:
time: 334 us; the launch traced here: 333 us
  waiting for transfers between devices  241 us (72%)
  starting transfers between devices  35.8 us (11%)
  matrix products  23.7 us (7%)
  between operations  14.9 us (4%)
  local copies, waits for them, and re-layouts  10.5 us (3%)
  other arithmetic  7.24 us (2%)
    unnamed x3, waiting for transfers between devices  132 us
    psum x1, waiting for transfers between devices, on_device(): totals = lax.psum(local_part, ('scene', 'row', 'col'))  96.1 us
    ppermute x6, starting transfers between devices, with_halo(): lax.ppermute(tail, axis, [(i, (i + 1) % count) for i in range(ends)])  18.6 us
    dot_general x18, matrix products, kernel_grad(): jnp.einsum('nhwc,nhwd->cd', window, errors, preferred_element_type=jnp.fl...  17 us
    ppermute x5, waiting for transfers between devices, on_device(): lax.ppermute(grown, ('scene', 'row', 'col'), [(d, d ^ reach) for d in ran...  11.7 us
    ppermute x5, starting transfers between devices, on_device(): lax.ppermute(grown, ('scene', 'row', 'col'), [(d, d ^ reach) for d in ran...  9.15 us
    ppermute x6, starting transfers between devices, with_halo(): lax.ppermute(head, axis, [((i + 1) % count, i) for i in range(ends)])  8.06 us
    unnamed x46, local copies, waits for them, and re-layouts  7.33 us
  transfers between devices with their start and end apart: 19, of which 6 were waited for; matrix products, arithmetic and copies ran while one was open for 6% of the time, Pallas kernels for 0%

profile of v1, /device:TPU:0, one launch (start us, length us, event | category | flops | bytes accessed | tf_op | source)
XLA Modules:
  0.0 332.9 jit_solution(14596863011184020188)
XLA Ops:
  8.1 4.9 %collective-permute-start = (bf16[1,1,64,128]{3,2,1,0:T(8,128)(2,1)S(1)}, bf16[1,1,64,128]{3,2,1,0:T(8,128)(2,1)S(1)}, u32[]{:S(2)}, u32[]{:S(2)}) collective-permute-start(bf16[1,1,64,128]{3,2,1,0:T(8,128)(2,1)S(1)} %get-tuple-element.18), channel_id=1, source_target_pairs={{0,2},{2,4},{4,6},{1,3},{3,5},{5,7},{8,10},{10,12},{12,14},{9,11},... | collective-permute-start | bytes 49160 | tf_op jit(solution)/shard_map/ppermute | solution.py:18
  15.0 4.5 %collective-permute-start.3 = (bf16[1,1,64,128]{3,2,1,0:T(8,128)(2,1)S(1)}, bf16[1,1,64,128]{3,2,1,0:T(8,128)(2,1)S(1)}, u32[]{:S(2)}, u32[]{:S(2)}) collective-permute-start(bf16[1,1,64,128]{3,2,1,0:T(8,128)(2,1)S(1)} %get-tuple-element.16), channel_id=1, source_target_pairs={{0,2},{2,4},{4,6},{1,3},{3,5},{5,7},{8,10},{10,12},{12,14},{9,11},... | collective-permute-start | bytes 49160 | tf_op jit(solution)/shard_map/ppermute | solution.py:18
  21.1 2.7 collective-permute-start.8
  23.9 2.5 collective-permute-done.8
  26.4 3.0 collective-permute-start.9
  30.8 3.0 collective-permute-start.2
  33.8 2.6 collective-permute-done.9
  36.4 1.5 collective-permute-start.10
  38.2 6.5 %collective-permute-done.10 = f32[73728]{0:T(1024)S(1)} collective-permute-done((f32[73728]{0:T(1024)S(1)}, f32[73728]{0:T(1024)S(1)}, u32[]{:S(2)}, u32[]{:S(2)}) %collective-permute-start.10) | collective-permute-done | bytes 294944 | tf_op jit(solution)/shard_map/ppermute | solution.py:63
  44.7 1.4 collective-permute-start.11
  53.5 96.1 %all-reduce.4.cloned.1.call-done = f32[294912]{0:T(1024)} async-done(((f32[294912]{0:T(1024)}), f32[294912]{0:T(1024)}) %all-reduce.4.cloned.1.call-update) | async-done | bytes 1179664 | tf_op jit(solution)/shard_map/psum | solution.py:59
  149.6 2.2 multiply_reduce_fusion
  152.5 1.5 fusion.16
  154.0 3.2 multiply_convert_fusion.1
  158.6 3.4 %multiply_convert_fusion = bf16[64,8,9,128]{3,1,2,0:T(8,128)(2,1)S(1)} fusion(f32[64,8,9,128]{3,1,2,0:T(8,128)S(1)} %get-tuple-element.22, bf16[3,3,128,128]{3,2,1,0:T(8,128)(2,1)S(1)} %bitcast.192, bf16[66,1,7,2,128]{4,2,3,0,1:T(8,128)(2,1)S(1)} %slice.173, bf16[66,1,8,9,128]{4,2,3,0,1:T(8,128)(2,1)S(1)} %copy-done.2, pred[8,9]{0,1:T(8,128)(4,1)S(1)} %copy-done.18), kind=kOutput, calls=%fused_computation.3 | convolution fusion | flops 1369903104 | bytes 5286984 | tf_op jit(solution)/shard_map/conv_general_dilated | solution.py:28
  165.0 3.5 %collective-permute-start.13 = (bf16[1,1,64,128]{3,2,1,0:T(8,128)(2,1)S(1)}, bf16[1,1,64,128]{3,2,1,0:T(8,128)(2,1)S(1)}, u32[]{:S(2)}, u32[]{:S(2)}) collective-permute-start(bf16[1,1,64,128]{3,2,1,0:T(8,128)(2,1)S(1)} %slice.186), channel_id=1, source_target_pairs={{0,2},{2,4},{4,6},{1,3},{3,5},{5,7},{8,10},{10,12},{12,14},{9,11},... | collective-permute-start | bytes 49160 | tf_op jit(solution)/shard_map/ppermute | solution.py:18
  168.6 1.6 collective-permute-start.14
  171.2 1.4 convolution_bitcast_fusion.11
  173.9 1.4 convolution_bitcast_fusion.9
  176.7 1.4 convolution_bitcast_fusion.12
  178.1 1.4 convolution_bitcast_fusion.17
  179.5 1.4 convolution_bitcast_fusion.15
  192.7 131.9 %all-reduce.6.cloned.1.call-done = f32[294912]{0:T(1024)} async-done(((f32[294912]{0:T(1024)}), f32[294912]{0:T(1024)}) %all-reduce.6.cloned.1.call-update) | async-done | bytes 1179664
  324.7 1.4 dynamic-slice
  (123 shorter events, 33.2 us)
Async XLA Ops:
  6.5 14.4 %copy-start.5 = (bf16[1,64,64,128]{3,2,1,0:T(8,128)(2,1)S(1)}, bf16[1,64,64,128]{3,2,1,0:T(8,128)(2,1)}, u32[]{:S(2)}) copy-start(bf16[1,64,64,128]{3,2,1,0:T(8,128)(2,1)} %param.4) | copy-start | bytes 3145732
  6.5 143.0 %all-reduce.4.cloned.1.call-start = ((), (), s32[]{:S(2)}) async-start(), calls=%async_computation | async-start | bytes 2359296 | tf_op jit(solution)/shard_map/psum | solution.py:59
  6.5 14.6 %collective-permute-start.7 = (f32[9216]{0:T(1024)}, f32[9216]{0:T(1024)S(1)}, u32[]{:S(2)}, u32[]{:S(2)}) collective-permute-start(f32[9216]{0:T(1024)} %param.6), channel_id=1, source_target_pairs={{0,1},{1,0},{2,3},{3,2},{4,5},{5,4},{6,7},{7,6},{8,9},{9,8},{10,11... | collective-permute-start | bytes 110600 | tf_op jit(solution)/shard_map/ppermute | solution.py:63
  7.3 13.9 %copy-start.11 = (f32[9216]{0:T(1024)S(1)}, f32[9216]{0:T(1024)}, u32[]{:S(2)}) copy-start(f32[9216]{0:T(1024)} %param.6) | copy-start | bytes 110596
  7.3 317.4 %all-reduce.6.cloned.1.call-start = ((), (), s32[]{:S(2)}) async-start(), calls=%async_computation.1 | async-start | bytes 2359296
  8.1 12.9 %collective-permute-start = (bf16[1,1,64,128]{3,2,1,0:T(8,128)(2,1)S(1)}, bf16[1,1,64,128]{3,2,1,0:T(8,128)(2,1)S(1)}, u32[]{:S(2)}, u32[]{:S(2)}) collective-permute-start(bf16[1,1,64,128]{3,2,1,0:T(8,128)(2,1)S(1)} %get-tuple-element.18), channel_id=1, source_target_pairs={{0,2},{2,4},{4,6},{1,3},{3,5},{5,7},{8,10},{10,12},{12,14},{9,11},... | collective-permute-start | bytes 49160 | tf_op jit(solution)/shard_map/ppermute | solution.py:18
  13.0 10.8 %collective-permute-start.1 = (bf16[1,1,64,128]{3,2,1,0:T(8,128)(2,1)S(1)}, bf16[1,1,64,128]{3,2,1,0:T(8,128)(2,1)S(1)}, u32[]{:S(2)}, u32[]{:S(2)}) collective-permute-start(bf16[1,1,64,128]{3,2,1,0:T(8,128)(2,1)S(1)} %get-tuple-element.17), channel_id=1, source_target_pairs={{2,0},{4,2},{6,4},{3,1},{5,3},{7,5},{10,8},{12,10},{14,12},{11,9},... | collective-permute-start | bytes 49160 | tf_op jit(solution)/shard_map/ppermute | solution.py:20
  15.0 22.9 %collective-permute-start.3 = (bf16[1,1,64,128]{3,2,1,0:T(8,128)(2,1)S(1)}, bf16[1,1,64,128]{3,2,1,0:T(8,128)(2,1)S(1)}, u32[]{:S(2)}, u32[]{:S(2)}) collective-permute-start(bf16[1,1,64,128]{3,2,1,0:T(8,128)(2,1)S(1)} %get-tuple-element.16), channel_id=1, source_target_pairs={{0,2},{2,4},{4,6},{1,3},{3,5},{5,7},{8,10},{10,12},{12,14},{9,11},... | collective-permute-start | bytes 49160 | tf_op jit(solution)/shard_map/ppermute | solution.py:18
  19.6 18.5 %collective-permute-start.4 = (bf16[1,1,64,128]{3,2,1,0:T(8,128)(2,1)S(1)}, bf16[1,1,64,128]{3,2,1,0:T(8,128)(2,1)S(1)}, u32[]{:S(2)}, u32[]{:S(2)}) collective-permute-start(bf16[1,1,64,128]{3,2,1,0:T(8,128)(2,1)S(1)} %get-tuple-element.15), channel_id=1, source_target_pairs={{2,0},{4,2},{6,4},{3,1},{5,3},{7,5},{10,8},{12,10},{14,12},{11,9},... | collective-permute-start | bytes 49160 | tf_op jit(solution)/shard_map/ppermute | solution.py:20
  20.9 17.0 %copy-start.7 = (bf16[1,64,64,128]{3,2,1,0:T(8,128)(2,1)S(1)}, bf16[1,64,64,128]{3,2,1,0:T(8,128)(2,1)}, u32[]{:S(2)}) copy-start(bf16[1,64,64,128]{3,2,1,0:T(8,128)(2,1)} %param.5) | copy-start | bytes 3145732
  21.1 5.2 %collective-permute-start.8 = (f32[18432]{0:T(1024)S(1)}, f32[18432]{0:T(1024)S(1)}, u32[]{:S(2)}, u32[]{:S(2)}) collective-permute-start(f32[18432]{0:T(1024)S(1)} %maximum_select_fusion.4), channel_id=1, source_target_pairs={{0,2},{1,3},{2,0},{3,1},{4,6},{5,7},{6,4},{7,5},{8,10},{9,11},{10,... | collective-permute-start | bytes 221192 | tf_op jit(solution)/shard_map/ppermute | solution.py:63
  23.9 14.3 %copy-start.16 = (bf16[1,1,64,128]{3,2,1,0:T(8,128)(2,1)}, bf16[1,1,64,128]{3,2,1,0:T(8,128)(2,1)S(1)}, u32[]{:S(2)}) copy-start(bf16[1,1,64,128]{3,2,1,0:T(8,128)(2,1)S(1)} %collective-permute-done.1) | copy-start | bytes 49156
  23.9 25.0 %copy-start.3 = (bf16[1,66,64,128]{3,2,1,0:T(8,128)(2,1)}, bf16[1,66,64,128]{3,2,1,0:T(8,128)(2,1)S(1)}, u32[]{:S(2)}) copy-start(bf16[1,66,64,128]{3,2,1,0:T(8,128)(2,1)S(1)} %constant_dynamic-update-slice_fusion) | copy-start | bytes 3244036
  26.4 10.0 %collective-permute-start.9 = (f32[36864]{0:T(1024)S(1)}, f32[36864]{0:T(1024)S(1)}, u32[]{:S(2)}, u32[]{:S(2)}) collective-permute-start(f32[36864]{0:T(1024)S(1)} %maximum_select_fusion.3), channel_id=1, source_target_pairs={{0,4},{1,5},{2,6},{3,7},{4,0},{5,1},{6,2},{7,3},{8,12},{9,13},{10,... | collective-permute-start | bytes 442376 | tf_op jit(solution)/shard_map/ppermute | solution.py:63
  29.5 19.4 %collective-permute-start.12 = (bf16[1,66,1,128]{3,2,1,0:T(2,128)(2,1)S(1)}, bf16[1,66,1,128]{3,2,1,0:T(2,128)(2,1)S(1)}, u32[]{:S(2)}, u32[]{:S(2)}) collective-permute-start(bf16[1,66,1,128]{3,2,1,0:T(2,128)(2,1)S(1)} %get-tuple-element.14), channel_id=1, source_target_pairs={{1,0},{3,2},{5,4},{7,6},{9,8},{11,10},{13,12},{15,14},{17,16},{19,... | collective-permute-start | bytes 50696 | tf_op jit(solution)/shard_map/ppermute | solution.py:20
  30.8 18.1 %collective-permute-start.2 = (bf16[1,66,1,128]{3,2,1,0:T(2,128)(2,1)S(1)}, bf16[1,66,1,128]{3,2,1,0:T(2,128)(2,1)S(1)}, u32[]{:S(2)}, u32[]{:S(2)}) collective-permute-start(bf16[1,66,1,128]{3,2,1,0:T(2,128)(2,1)S(1)} %get-tuple-element.13), channel_id=1, source_target_pairs={{0,1},{2,3},{4,5},{6,7},{8,9},{10,11},{12,13},{14,15},{16,17},{18,... | collective-permute-start | bytes 50696 | tf_op jit(solution)/shard_map/ppermute | solution.py:18
  36.4 8.3 %collective-permute-start.10 = (f32[73728]{0:T(1024)S(1)}, f32[73728]{0:T(1024)S(1)}, u32[]{:S(2)}, u32[]{:S(2)}) collective-permute-start(f32[73728]{0:T(1024)S(1)} %maximum_select_fusion.2), channel_id=1, source_target_pairs={{0,8},{1,9},{2,10},{3,11},{4,12},{5,13},{6,14},{7,15},{8,0},{9,1},... | collective-permute-start | bytes 884744 | tf_op jit(solution)/shard_map/ppermute | solution.py:63
  44.7 107.7 %collective-permute-start.11 = (f32[147456]{0:T(1024)S(1)}, f32[147456]{0:T(1024)}, u32[]{:S(2)}, u32[]{:S(2)}) collective-permute-start(f32[147456]{0:T(1024)S(1)} %maximum_select_fusion.1), channel_id=1, source_target_pairs={{0,16},{1,17},{2,18},{3,19},{4,20},{5,21},{6,22},{7,23},{8,24},{9,... | collective-permute-start | bytes 1769480 | tf_op jit(solution)/shard_map/ppermute | solution.py:63
  46.2 5.0 %collective-permute-start.5 = (bf16[1,66,1,128]{3,2,1,0:T(2,128)(2,1)S(1)}, bf16[1,66,1,128]{3,2,1,0:T(2,128)(2,1)S(1)}, u32[]{:S(2)}, u32[]{:S(2)}) collective-permute-start(bf16[1,66,1,128]{3,2,1,0:T(2,128)(2,1)S(1)} %get-tuple-element.7), channel_id=1, source_target_pairs={{0,1},{2,3},{4,5},{6,7},{8,9},{10,11},{12,13},{14,15},{16,17},{18,... | collective-permute-start | bytes 50696 | tf_op jit(solution)/shard_map/ppermute | solution.py:18
  47.5 3.7 %collective-permute-start.6 = (bf16[1,66,1,128]{3,2,1,0:T(2,128)(2,1)S(1)}, bf16[1,66,1,128]{3,2,1,0:T(2,128)(2,1)S(1)}, u32[]{:S(2)}, u32[]{:S(2)}) collective-permute-start(bf16[1,66,1,128]{3,2,1,0:T(2,128)(2,1)S(1)} %get-tuple-element.8), channel_id=1, source_target_pairs={{1,0},{3,2},{5,4},{7,6},{9,8},{11,10},{13,12},{15,14},{17,16},{19,... | collective-permute-start | bytes 50696 | tf_op jit(solution)/shard_map/ppermute | solution.py:20
  165.0 18.2 %collective-permute-start.13 = (bf16[1,1,64,128]{3,2,1,0:T(8,128)(2,1)S(1)}, bf16[1,1,64,128]{3,2,1,0:T(8,128)(2,1)S(1)}, u32[]{:S(2)}, u32[]{:S(2)}) collective-permute-start(bf16[1,1,64,128]{3,2,1,0:T(8,128)(2,1)S(1)} %slice.186), channel_id=1, source_target_pairs={{0,2},{2,4},{4,6},{1,3},{3,5},{5,7},{8,10},{10,12},{12,14},{9,11},... | collective-permute-start | bytes 49160 | tf_op jit(solution)/shard_map/ppermute | solution.py:18
  168.6 14.6 %collective-permute-start.14 = (bf16[1,1,64,128]{3,2,1,0:T(8,128)(2,1)S(1)}, bf16[1,1,64,128]{3,2,1,0:T(8,128)(2,1)S(1)}, u32[]{:S(2)}, u32[]{:S(2)}) collective-permute-start(bf16[1,1,64,128]{3,2,1,0:T(8,128)(2,1)S(1)} %slice.189), channel_id=1, source_target_pairs={{2,0},{4,2},{6,4},{3,1},{5,3},{7,5},{10,8},{12,10},{14,12},{11,9},... | collective-permute-start | bytes 49160 | tf_op jit(solution)/shard_map/ppermute | solution.py:20
  183.3 3.6 %collective-permute-start.15 = (bf16[1,66,1,128]{3,2,1,0:T(2,128)(2,1)S(1)}, bf16[1,66,1,128]{3,2,1,0:T(2,128)(2,1)S(1)}, u32[]{:S(2)}, u32[]{:S(2)}) collective-permute-start(bf16[1,66,1,128]{3,2,1,0:T(2,128)(2,1)S(1)} %get-tuple-element.11), channel_id=1, source_target_pairs={{0,1},{2,3},{4,5},{6,7},{8,9},{10,11},{12,13},{14,15},{16,17},{18,... | collective-permute-start | bytes 50696 | tf_op jit(solution)/shard_map/ppermute | solution.py:18
  184.6 3.1 collective-permute-start.16
  (14 other events, 26.3 us)
Sparse Core Ops, SparseCore 0:
  12.7 136.7 all-reduce.3
  192.8 131.7 all-reduce.5
